TPU v7x, 512 devices: a whole 4x4x16 slice. The times are simulated.
512 devices in a mesh: seq: 32 (over z, core), head: 16 (over x, y).
Axes of the slice: x: 4, y: 4, z: 16, core: 2. Of those that a mesh axis runs over, the one named last changes fastest.
Arguments:
- tokens: bfloat16 [8192, 4096], P('seq', 'head'), may hold values from -40 to 40
- norm_gain: float32 [4096], replicated, may hold values from 1.5 to 8
- w_qkv: bfloat16 [4096, 3, 2048], P(None, None, 'head'), may hold values from -0.09375 to 0.09375
- w_out: bfloat16 [2048, 4096], P('head'), may hold values from -0.75 to 0.75
- span_order: int32 [64], replicated, may hold values from 0 to 63, each once
- frame_id: int32 [8192], replicated, may hold values from 0 to 63, never falling along the last dimension, each value on 1 to 256 neighbouring positions
- camera_id: int32 [8192], replicated, may hold values from 0 to 5
Outputs:
- mixed: bfloat16 [8192, 4096], P('seq', 'head')
Inputs may be any that keep to these rules, and one draw needn't show every extreme that they name: `span_order`: each of the 64 spans appears once. `frame_id`: never falls along the sequence; every frame has 1 to 256 positions and one has exactly 256.
All inputs are finite; a program needn't handle non-finite values.
Results may differ from a plain program's by a relative error of at most 0.015.
The roundings to bfloat16 on the way count: a program that leaves them out, or rounds other values in their place, can miss the bound.
Values may be sent and summed in bfloat16 or wider, within the bound.
No kernel may reach another device: no remote copies, remote signals or barrier semaphores. Data moves between devices by JAX's collectives and lax.ppermute only.
A program may use at most 64 MiB of HBM per device.

v0:
```python
import jax
import jax.numpy as jnp
from jax import lax
from jax.sharding import PartitionSpec as P

D = 4096
HD = 128
epsilon = 1e-06
key_block = 1024


def stored_order(id_table, span_order):
    span_count = span_order.shape[0]
    return id_table.reshape(span_count, -1)[span_order].reshape(-1)


def visible_pairs(query_frames, query_cameras, key_frames, key_cameras):
    earlier = key_frames[None, :] < query_frames[:, None]
    same_view = (key_frames[None, :] == query_frames[:, None]) & (
        key_cameras[None, :] == query_cameras[:, None]
    )
    return earlier | same_view


def on_device(tokens, norm_gain, w_qkv, w_out, span_order, frame_id, camera_id):
    gathered = lax.all_gather(tokens, "head", axis=1, tiled=True)
    widened = gathered.astype(jnp.float32)
    inverse = lax.rsqrt(jnp.mean(widened * widened, axis=1, keepdims=True) + epsilon)
    normed = (widened * inverse * norm_gain).astype(jnp.bfloat16)
    row_count = tokens.shape[0]
    local_heads = w_out.shape[0] // HD
    projected = jnp.dot(
        normed, w_qkv.reshape(D, 3 * local_heads * HD), preferred_element_type=jnp.float32
    )
    projected = projected.astype(jnp.bfloat16).reshape(row_count, 3, local_heads, HD)
    queries = projected[:, 0]
    key_rows = projected[:, 1].reshape(row_count, local_heads * HD)
    value_rows = projected[:, 2].reshape(row_count, local_heads * HD)
    frames = stored_order(frame_id, span_order)
    cameras = stored_order(camera_id, span_order)
    first_row = lax.axis_index("seq") * row_count
    query_frames = lax.dynamic_slice_in_dim(frames, first_row, row_count, 0)
    query_cameras = lax.dynamic_slice_in_dim(cameras, first_row, row_count, 0)
    score_scale = HD ** (-0.5)

    def absorb(running, block_keys, block_values, key_start, frame_table, camera_table):
        key_count = block_keys.shape[0]
        key_frames = lax.dynamic_slice_in_dim(frame_table, key_start, key_count, 0)
        key_cameras = lax.dynamic_slice_in_dim(camera_table, key_start, key_count, 0)
        old_best, running_total, weighted = running
        scores = (
            jnp.einsum(
                "qhd,khd->hqk",
                queries,
                block_keys.reshape(key_count, local_heads, HD),
                preferred_element_type=jnp.float32,
            )
            * score_scale
        )
        allowed = visible_pairs(query_frames, query_cameras, key_frames, key_cameras)[None]
        block_best = jnp.max(jnp.where(allowed, scores, -jnp.inf), axis=2)
        new_best = jnp.maximum(old_best, block_best)
        weights = jnp.exp(jnp.where(allowed, scores - new_best[:, :, None], -jnp.inf))
        factor = jnp.exp(old_best - new_best)
        running_total = running_total * factor + jnp.sum(weights, axis=2)
        added = jnp.einsum(
            "hqk,khd->hqd",
            weights.astype(jnp.bfloat16),
            block_values.reshape(key_count, local_heads, HD),
            preferred_element_type=jnp.float32,
        )
        weighted = weighted * factor[:, :, None] + added
        return (new_best, running_total, weighted)

    initial = (
        jnp.full((local_heads, row_count), -1e30, jnp.float32),
        jnp.zeros((local_heads, row_count), jnp.float32),
        jnp.zeros((local_heads, row_count, HD), jnp.float32),
    )
    all_keys, all_values = (
        lax.all_gather(key_rows, "seq", axis=0, tiled=True),
        lax.all_gather(value_rows, "seq", axis=0, tiled=True),
    )
    running = initial
    length = all_keys.shape[0]
    block_rows = min(key_block, length)
    full_blocks = length // block_rows

    def advance(block_index, current):
        offset = block_index * block_rows
        block_keys = lax.dynamic_slice_in_dim(all_keys, offset, block_rows, 0)
        block_values = lax.dynamic_slice_in_dim(all_values, offset, block_rows, 0)
        return absorb(current, block_keys, block_values, 0 + offset, frames, cameras)

    running = lax.fori_loop(0, full_blocks, advance, running)
    attended = (running[2] / running[1][:, :, None]).astype(jnp.bfloat16)
    partial_value = jnp.einsum(
        "hqd,hde->qe",
        attended,
        w_out.reshape(local_heads, HD, D),
        preferred_element_type=jnp.float32,
    )
    mixed_rows = lax.psum_scatter(
        partial_value.astype(jnp.bfloat16), "head", scatter_dimension=1, tiled=True
    )
    return mixed_rows


def solution(mesh):
    placed = (P("seq", "head"), P(), P(None, None, "head"), P("head", None), P(), P(), P())
    return jax.shard_map(
        on_device, mesh=mesh, in_specs=placed, out_specs=P("seq", "head"), check_vma=False
    )
```

profile of v0, /device:TPU:2, one launch (start us, length us, event | category | flops | bytes accessed | tf_op | source)
XLA Modules:
  0.0 355.3 jit_solution(11500444099656653798)
XLA Ops:
  6.5 0.7 all-gather.6.cloned.1.call-update
  7.3 4.7 %copy.11 = bf16[4096,3,128]{0,2,1:T(8,128)(2,1)} copy(bf16[4096,3,128]{2,0,1:T(8,128)(2,1)} %param.11) | data formatting | bytes 6291456 | tf_op args[2]
  12.0 64.8 %all-gather.6.cloned.1.call-done = bf16[256,4096]{1,0:T(8,128)(2,1)} async-done(((bf16[256,256]{1,0:T(8,128)(2,1)}), bf16[256,4096]{1,0:T(8,128)(2,1)}) %all-gather.6.cloned.1.call-update) | async-done | bytes 2097168 | tf_op jit(solution)/shard_map/all_gather | solution.py:26
  76.8 2.2 fusion.16
  79.1 3.3 fusion.23
  83.3 0.7 all-gather.8.cloned.1.call-update
  85.6 70.4 %all-gather.10.cloned.1.call-done = bf16[8192,1,1,128]{0,3,1,2:T(8,128)(2,1)} async-done(((bf16[256,1,1,128]{0,3,1,2:T(8,128)(2,1)}), bf16[8192,1,1,128]{0,3,1,2:T(8,128)(2,1)}) %all-gather.10.cloned.1.call-update) | async-done | bytes 2097168 | tf_op jit(solution)/shard_map/all_gather | solution.py:82
  156.0 70.8 %all-gather.8.cloned.1.call-done = bf16[8192,1,1,128]{0,3,1,2:T(8,128)(2,1)} async-done(((bf16[256,1,1,128]{0,3,1,2:T(8,128)(2,1)}), bf16[8192,1,1,128]{0,3,1,2:T(8,128)(2,1)}) %all-gather.8.cloned.1.call-update) | async-done | bytes 2097168 | tf_op jit(solution)/shard_map/all_gather | solution.py:81
  226.8 33.6 %while.18 = (s32[]{:T(128)}, f32[1,256]{1,0:T(1,128)S(1)}, f32[1,256]{1,0:T(1,128)S(1)}, f32[1,256,128]{2,1,0:T(8,128)S(1)}, s32[8192]{0:T(1024)S(1)}, /*index=5...) while((s32[]{:T(128)}, f32[1,256]{1,0:T(1,128)S(1)}, ...), condition=%wide.region_4.5_spmd.clone, body=%wide.region_1.4_spmd.clone.sunk | while | flops 140608768 | bytes 4061407 | solution.py:95
  226.8 1.7 select_reduce_fusion.2
  229.3 1.7 fusion.41
  231.0 1.8 select_reduce_fusion.2
  233.5 1.7 fusion.41
  235.3 1.8 select_reduce_fusion.2
  237.0 0.7 fusion.39
  237.7 1.7 fusion.41
  239.5 1.8 select_reduce_fusion.2
  241.3 0.7 fusion.39
  242.0 1.7 fusion.41
  243.7 1.8 select_reduce_fusion.2
  245.5 0.7 fusion.39
  246.2 1.7 fusion.41
  247.9 1.8 select_reduce_fusion.2
  249.7 0.7 fusion.39
  250.4 1.7 fusion.41
  252.1 1.8 select_reduce_fusion.2
  253.9 0.7 fusion.39
  254.6 1.7 fusion.41
  256.3 1.8 select_reduce_fusion.2
  258.8 1.7 fusion.41
  260.5 2.1 convolution_convert_fusion
  262.6 86.2 %reduce-scatter.2.cloned.1.call-done = bf16[256,256]{1,0:T(8,128)(2,1)} async-done(((bf16[256,4096]{1,0:T(8,128)(2,1)}), bf16[256,256]{1,0:T(8,128)(2,1)}) %reduce-scatter.2.cloned.1.call-update) | async-done | bytes 131088 | tf_op jit(solution)/shard_map/reduce_scatter | solution.py:103
  (74 shorter events, 4.9 us)
Async XLA Ops:
  6.5 254.0 %copy-start = (bf16[128,4096]{1,0:T(8,128)(2,1)S(1)}, bf16[128,4096]{1,0:T(8,128)(2,1)}, u32[]{:S(2)}) copy-start(bf16[128,4096]{1,0:T(8,128)(2,1)} %param.12) | copy-start | bytes 3145732
  6.5 70.3 %all-gather.6.cloned.1.call-start = ((), (), s32[]{:S(2)}) async-start(), calls=%async_computation.1 | async-start | bytes 2228224 | tf_op jit(solution)/shard_map/all_gather | solution.py:26
  7.3 148.8 %all-gather.10.cloned.1.call-start = ((), (), s32[]{:S(2)}) async-start(), calls=%async_computation.4 | async-start | bytes 2162688 | tf_op jit(solution)/shard_map/all_gather | solution.py:82
  7.3 71.7 %copy-start.4 = (f32[4096]{0:T(1024)S(1)}, f32[4096]{0:T(1024)}, u32[]{:S(2)}) copy-start(f32[4096]{0:T(1024)} %param.10) | copy-start | bytes 49156
  76.8 2.3 copy-start.3
  79.1 5.0 %copy-start.5 = (s32[64]{0:T(128)S(1)}, s32[64]{0:T(128)}, u32[]{:S(2)}) copy-start(s32[64]{0:T(128)} %param.13) | copy-start | bytes 772
  79.1 5.0 %copy-start.1 = (s32[8192]{0:T(1024)S(1)}, s32[8192]{0:T(1024)}, u32[]{:S(2)}) copy-start(s32[8192]{0:T(1024)} %param.15) | copy-start | bytes 98308
  79.1 5.6 %copy-start.2 = (s32[8192]{0:T(1024)S(1)}, s32[8192]{0:T(1024)}, u32[]{:S(2)}) copy-start(s32[8192]{0:T(1024)} %param.14) | copy-start | bytes 98308
  83.3 143.6 %all-gather.8.cloned.1.call-start = ((), (), s32[]{:S(2)}) async-start(), calls=%async_computation.3 | async-start | bytes 2162688 | tf_op jit(solution)/shard_map/all_gather | solution.py:81
  84.0 264.8 %reduce-scatter.2.cloned.1.call-start = ((), (), s32[]{:S(2)}) async-start(), calls=%async_computation.2 | async-start | bytes 2228224 | tf_op jit(solution)/shard_map/reduce_scatter | solution.py:103
Sparse Core Ops, SparseCore 0:
  10.3 66.4 all-gather.5
  83.4 72.6 all-gather.9
  158.1 68.7 all-gather.7
  262.7 86.0 reduce-scatter.1
where the time goes:
time: 356 us; the launch traced here: 355 us
  waiting for transfers between devices  294 us (83%)
  matrix products  32.7 us (9%)
  between operations  13.3 us (4%)
  other arithmetic  7.89 us (2%)
  local copies, waits for them, and re-layouts  7.13 us (2%)
    reduce_scatter x1, waiting for transfers between devices, on_device(): lax.psum_scatter(partial_value.astype(jnp.bfloat16), 'head', scatter_dime...  86.2 us
    all_gather x1, waiting for transfers between devices, on_device(): lax.all_gather(key_rows, 'seq', axis=0, tiled=True)  70.8 us
    all_gather x1, waiting for transfers between devices, on_device(): lax.all_gather(value_rows, 'seq', axis=0, tiled=True)  70.4 us
    all_gather x1, waiting for transfers between devices, on_device(): gathered = lax.all_gather(tokens, 'head', axis=1, tiled=True)  64.8 us
    dot_general x8, matrix products, absorb(): jnp.einsum('qhd,khd->hqk', queries, block_keys.reshape(key_count, local_h...  14.1 us
    dot_general x8, matrix products, absorb(): jnp.einsum('hqk,khd->hqd', weights.astype(jnp.bfloat16), block_values.res...  13.2 us
  transfers between devices with their start and end apart: 4, of which 4 were waited for; matrix products, arithmetic and copies ran while one was open for 2% of the time, Pallas kernels for 0%

commit v1 on v0

--- a/solution.py
+++ b/solution.py
@@ -23,7 +23,10 @@
 
 
 def on_device(tokens, norm_gain, w_qkv, w_out, span_order, frame_id, camera_id):
-    gathered = lax.all_gather(tokens, "head", axis=1, tiled=True)
+    size = lax.axis_size("head")
+    pieces = jnp.stack([tokens for _ in range(size)])
+    pieces = lax.all_to_all(pieces, "head", split_axis=0, concat_axis=0)
+    gathered = jnp.concatenate(pieces, axis=1)
     widened = gathered.astype(jnp.float32)
     inverse = lax.rsqrt(jnp.mean(widened * widened, axis=1, keepdims=True) + epsilon)
     normed = (widened * inverse * norm_gain).astype(jnp.bfloat16)

time: 356 us -> 325 us (0.913)
  waiting for transfers between devices: 294 us -> 253 us
  starting transfers between devices: 0.12 us -> 9.65 us
  local copies, waits for them, and re-layouts: 7.13 us -> 10.9 us
    all_gather x1 -> x0, waiting for transfers between devices: 64.8 us -> none  [on_device(): gathered = lax.all_gather(tokens, 'head', axis=1, tiled=True)]
    all_to_all x0 -> x1, waiting for transfers between devices: none -> 20.6 us  [on_device(): pieces = lax.all_to_all(pieces, 'head', split_axis=0, concat_axis=0)]
    all_to_all x0 -> x1, starting transfers between devices: none -> 9.54 us  [on_device(): pieces = lax.all_to_all(pieces, 'head', split_axis=0, concat_axis=0)]
    all_gather x1, waiting for transfers between devices: 70.4 us -> 74.3 us  [on_device(): lax.all_gather(value_rows, 'seq', axis=0, tiled=True)]
where the time goes in v1:
time: 325 us
  waiting for transfers between devices  253 us (78%)
  matrix products  30.7 us (9%)
  between operations  13.3 us (4%)
  local copies, waits for them, and re-layouts  10.9 us (3%)
  starting transfers between devices  9.65 us (3%)
  other arithmetic  6.95 us (2%)
    reduce_scatter x1, waiting for transfers between devices, on_device(): lax.psum_scatter(partial_value.astype(jnp.bfloat16), 'head', scatter_dime...  86.3 us
    all_gather x1, waiting for transfers between devices, on_device(): lax.all_gather(value_rows, 'seq', axis=0, tiled=True)  74.3 us
    all_gather x1, waiting for transfers between devices, on_device(): lax.all_gather(key_rows, 'seq', axis=0, tiled=True)  70.8 us
    all_to_all x1, waiting for transfers between devices, on_device(): pieces = lax.all_to_all(pieces, 'head', split_axis=0, concat_axis=0)  20.6 us
    dot_general x8, matrix products, absorb(): jnp.einsum('qhd,khd->hqk', queries, block_keys.reshape(key_count, local_h...  14.1 us
    dot_general x8, matrix products, absorb(): jnp.einsum('hqk,khd->hqd', weights.astype(jnp.bfloat16), block_values.res...  13.2 us
    all_to_all x1, starting transfers between devices, on_device(): pieces = lax.all_to_all(pieces, 'head', split_axis=0, concat_axis=0)  9.54 us
    unnamed x14, local copies, waits for them, and re-layouts  6.99 us
  transfers between devices with their start and end apart: 4, of which 4 were waited for; matrix products, arithmetic and copies ran while one was open for 2% of the time, Pallas kernels for 0%

profile of v1, /device:TPU:2, one launch (start us, length us, event | category | flops | bytes accessed | tf_op | source)
XLA Modules:
  0.0 324.7 jit_solution(229078291699532727)
XLA Ops:
  6.5 1.1 copy.11
  7.6 1.5 stack.2
  9.2 9.5 %all-to-all-start = ((bf16[16,256,256]{1,2,0:T(8,128)(2,1)}), bf16[16,256,256]{1,2,0:T(8,128)(2,1)S(1)}, u32[]{:S(2)}, u32[]{:S(2)}) async-start(bf16[16,256,256]{1,2,0:T(8,128)(2,1)} %stack.2), calls=%async_computation | async-start | bytes 4194304 | tf_op jit(solution)/shard_map/all_to_all | solution.py:28
  18.8 4.7 %copy.12 = bf16[4096,3,128]{0,2,1:T(8,128)(2,1)} copy(bf16[4096,3,128]{2,0,1:T(8,128)(2,1)} %param.11) | data formatting | bytes 6291456 | tf_op args[2]
  23.5 20.6 %all-to-all-done = bf16[16,256,256]{1,2,0:T(8,128)(2,1)S(1)} async-done(((bf16[16,256,256]{1,2,0:T(8,128)(2,1)}), bf16[16,256,256]{1,2,0:T(8,128)(2,1)S(1)}, u32[]{:S(2)}, u32[]{:S(2)}) %all-to-all-start) | async-done | bytes 2097184 | tf_op jit(solution)/shard_map/all_to_all | solution.py:28
  44.7 0.7 fusion.18
  45.4 1.2 copy-done.1
  46.6 1.3 convolution_convert_fusion.1
  48.7 0.7 all-gather.5.cloned.1.call-update
  51.0 74.3 %all-gather.7.cloned.1.call-done = bf16[8192,1,1,128]{0,3,1,2:T(8,128)(2,1)} async-done(((bf16[256,1,1,128]{0,3,1,2:T(8,128)(2,1)}), bf16[8192,1,1,128]{0,3,1,2:T(8,128)(2,1)}) %all-gather.7.cloned.1.call-update) | async-done | bytes 2097168 | tf_op jit(solution)/shard_map/all_gather | solution.py:85
  125.4 70.8 %all-gather.5.cloned.1.call-done = bf16[8192,1,1,128]{0,3,1,2:T(8,128)(2,1)} async-done(((bf16[256,1,1,128]{0,3,1,2:T(8,128)(2,1)}), bf16[8192,1,1,128]{0,3,1,2:T(8,128)(2,1)}) %all-gather.5.cloned.1.call-update) | async-done | bytes 2097168 | tf_op jit(solution)/shard_map/all_gather | solution.py:84
  196.2 33.6 %while.18 = (s32[]{:T(128)}, f32[1,256]{1,0:T(1,128)S(1)}, f32[1,256]{1,0:T(1,128)S(1)}, f32[1,256,128]{2,1,0:T(8,128)S(1)}, s32[8192]{0:T(1024)S(1)}, /*index=5...) while((s32[]{:T(128)}, f32[1,256]{1,0:T(1,128)S(1)}, ...), condition=%wide.region_4.5_spmd.clone, body=%wide.region_1.4_spmd.clone.sunk | while | flops 140608768 | bytes 4061407 | solution.py:98
  196.2 1.7 select_reduce_fusion.2
  197.9 0.7 fusion.33
  198.6 1.7 fusion.35
  200.4 1.8 select_reduce_fusion.2
  202.2 0.7 fusion.33
  202.9 1.7 fusion.35
  204.6 1.8 select_reduce_fusion.2
  207.1 1.7 fusion.35
  208.8 1.8 select_reduce_fusion.2
  211.3 1.7 fusion.35
  213.0 1.8 select_reduce_fusion.2
  215.5 1.7 fusion.35
  217.2 1.8 select_reduce_fusion.2
  219.7 1.7 fusion.35
  221.4 1.8 select_reduce_fusion.2
  223.9 1.7 fusion.35
  225.6 1.8 select_reduce_fusion.2
  228.1 1.7 fusion.35
  229.8 2.1 convolution_convert_fusion
  231.9 86.3 %reduce-scatter.2.cloned.1.call-done = bf16[256,256]{1,0:T(8,128)(2,1)} async-done(((bf16[256,4096]{1,0:T(8,128)(2,1)}), bf16[256,256]{1,0:T(8,128)(2,1)}) %reduce-scatter.2.cloned.1.call-update) | async-done | bytes 131088 | tf_op jit(solution)/shard_map/reduce_scatter | solution.py:106
  (77 shorter events, 7.5 us)
Async XLA Ops:
  6.5 223.3 %copy-start = (bf16[128,4096]{1,0:T(8,128)(2,1)S(1)}, bf16[128,4096]{1,0:T(8,128)(2,1)}, u32[]{:S(2)}) copy-start(bf16[128,4096]{1,0:T(8,128)(2,1)} %param.12) | copy-start | bytes 3145732
  9.2 9.6 %copy-start.4 = (f32[4096]{0:T(1024)S(1)}, f32[4096]{0:T(1024)}, u32[]{:S(2)}) copy-start(f32[4096]{0:T(1024)} %param.10) | copy-start | bytes 49156
  9.2 34.9 %all-to-all-start = ((bf16[16,256,256]{1,2,0:T(8,128)(2,1)}), bf16[16,256,256]{1,2,0:T(8,128)(2,1)S(1)}, u32[]{:S(2)}, u32[]{:S(2)}) async-start(bf16[16,256,256]{1,2,0:T(8,128)(2,1)} %stack.2), calls=%async_computation | async-start | bytes 4194304 | tf_op jit(solution)/shard_map/all_to_all | solution.py:28
  18.7 106.7 %all-gather.7.cloned.1.call-start = ((), (), s32[]{:S(2)}) async-start(), calls=%async_computation.4 | async-start | bytes 2162688 | tf_op jit(solution)/shard_map/all_gather | solution.py:85
  44.7 1.9 copy-start.1
  46.6 3.0 copy-start.5
  46.6 3.0 copy-start.2
  46.6 3.6 %copy-start.3 = (s32[8192]{0:T(1024)S(1)}, s32[8192]{0:T(1024)}, u32[]{:S(2)}) copy-start(s32[8192]{0:T(1024)} %param.14) | copy-start | bytes 98308
  48.7 147.5 %all-gather.5.cloned.1.call-start = ((), (), s32[]{:S(2)}) async-start(), calls=%async_computation.3 | async-start | bytes 2162688 | tf_op jit(solution)/shard_map/all_gather | solution.py:84
  49.4 268.8 %reduce-scatter.2.cloned.1.call-start = ((), (), s32[]{:S(2)}) async-start(), calls=%async_computation.2 | async-start | bytes 2228224 | tf_op jit(solution)/shard_map/reduce_scatter | solution.py:106
Sparse Core Ops, SparseCore 0:
  48.8 76.5 all-gather.6
  127.4 68.7 all-gather.4
  232.1 86.0 reduce-scatter.1
